TPU v7x, 32 devices: a whole 2x2x4 slice. The times are simulated.
32 devices in a mesh: section: 2 (over y), blk: 8 (over z, x), mp: 2 (over core).
Axes of the slice: x: 2, y: 2, z: 4, core: 2. Of those that a mesh axis runs over, the one named last changes fastest.
Arguments:
- queries: bfloat16 [2, 1024, 4096], P('section', 'blk', 'mp'), may hold values from -210 to 210
- encoder_states: bfloat16 [512, 2048], P(('blk', 'section', 'mp')), may hold values from -200 to 200
- norm_gain: float32 [2048], replicated, may hold values from 0.25 to 1.75
- kv_weight: bfloat16 [2, 2048, 2, 512], P('section', 'blk', None, 'mp'), may hold values from -0.125 to 0.125
- span_len: int32 [64], replicated, may hold values from 1 to 57, as said below
- span_owner: int32 [64], replicated, may hold values from 0 to 7, as said below
Outputs:
- attended: bfloat16 [2, 1024, 4096], P('section', 'blk', 'mp')
Inputs may be any that keep to these rules, and one draw needn't show every extreme that they name: `span_owner`: each span lies whole in the slots of one blk index; each blk index owns exactly 8 spans. `span_len`: the spans of one blk index hold at most 64 tokens together, exactly 64 for some blk index in every draw; all spans hold 288 tokens together; one span holds exactly 57 tokens in every draw.
All inputs are finite; a program needn't handle non-finite values.
Results may differ from a plain program's by a relative error of at most 0.0094.
Values may be sent and summed in bfloat16 or wider, within the bound.
No kernel may reach another device: no remote copies, remote signals or barrier semaphores. Data moves between devices by JAX's collectives and lax.ppermute only.
A program may use at most 64 MiB of HBM per device.

v0:
```python
import jax
import jax.numpy as jnp
from jax import lax
from jax.sharding import PartitionSpec as P

HEADS = 32
KVH = 4
HD = 128


def normalize(states, norm_gain):
    widened = states.astype(jnp.float32)
    factor = lax.rsqrt(jnp.mean(widened * widened, axis=-1, keepdims=True) + 1e-05)
    return (widened * factor * norm_gain).astype(jnp.bfloat16)


def slot_loads(span_len, span_owner, block_count):
    owners = span_owner[:, None] == jnp.arange(block_count, dtype=jnp.int32)[None, :]
    return jnp.sum(jnp.where(owners, span_len[:, None], 0), axis=0)


def live_slots(slot_load, row_count, capacity):
    slot_ids = jnp.arange(row_count, dtype=jnp.int32)
    holder = slot_ids // capacity
    picked = holder[:, None] == jnp.arange(slot_load.shape[0], dtype=jnp.int32)[None, :]
    holder_load = jnp.sum(jnp.where(picked, slot_load[None, :], 0), axis=1)
    return slot_ids % capacity < holder_load


def attend_block(state_now, query_grid, key_rows, value_rows, alive):
    running_max, denominator, numerator = state_now
    row_count = key_rows.shape[0]
    groups = query_grid.shape[1]
    head_size = query_grid.shape[3]
    key_grid = key_rows.reshape(row_count, groups, head_size)
    value_grid = value_rows.reshape(row_count, groups, head_size)
    scores = jnp.einsum(
        "qgjd,rgd->qgjr", query_grid, key_grid, preferred_element_type=jnp.float32
    ) * head_size ** (-0.5)
    scores = jnp.where(alive, scores, -1e30)
    new_max = jnp.maximum(running_max, jnp.max(scores, axis=-1))
    weights = jnp.where(alive, jnp.exp(scores - new_max[..., None]), 0.0)
    denominator = jnp.sum(weights, axis=-1)
    numerator = jnp.einsum(
        "qgjr,rgd->qgjd",
        weights.astype(jnp.bfloat16),
        value_grid,
        preferred_element_type=jnp.float32,
    )
    return (new_max, denominator, numerator)


def attend(state_now, query_grid, key_rows, value_rows, slot_load, capacity):
    row_count = key_rows.shape[0]
    alive = live_slots(slot_load, row_count, capacity)
    return attend_block(state_now, query_grid, key_rows, value_rows, alive)


def local(queries, encoder_states, norm_gain, kv_weight, span_len, span_owner):
    gathered = lax.all_gather(encoder_states, ("section", "mp"), axis=0, tiled=True)
    capacity = gathered.shape[0]
    normed = normalize(gathered, norm_gain)
    block_count = lax.axis_size("blk")
    slot_load = slot_loads(span_len, span_owner, block_count)
    group_width = kv_weight.shape[3]
    local_groups = group_width // HD
    group_size = HEADS // KVH
    query_rows = queries.shape[1]
    query_grid = queries[0].reshape(query_rows, local_groups, group_size, HD)
    start_state = (
        jnp.full((query_rows, local_groups, group_size), -1e30, jnp.float32),
        jnp.zeros((query_rows, local_groups, group_size), jnp.float32),
        jnp.zeros((query_rows, local_groups, group_size, HD), jnp.float32),
    )
    projected = jnp.einsum(
        "cr,rtk->ctk",
        normed,
        lax.all_gather(kv_weight, "blk", axis=1, tiled=True)[0],
        preferred_element_type=jnp.float32,
    )
    key_rows = projected[:, 0].astype(jnp.bfloat16)
    value_rows = projected[:, 1].astype(jnp.bfloat16)
    final_state = attend(
        start_state,
        query_grid,
        lax.all_gather(key_rows, "blk", axis=0, tiled=True),
        lax.all_gather(value_rows, "blk", axis=0, tiled=True),
        slot_load,
        capacity,
    )
    denominator = final_state[1]
    numerator = final_state[2]
    attended = (numerator / denominator[..., None]).astype(jnp.bfloat16)
    return attended.reshape(1, query_rows, local_groups * group_size * HD)


def solution(mesh):
    in_specs = (
        P("section", "blk", "mp"),
        P(("blk", "section", "mp"), None),
        P(),
        P("section", "blk", None, "mp"),
        P(),
        P(),
    )
    out_specs = P("section", "blk", "mp")
    return jax.shard_map(local, mesh=mesh, in_specs=in_specs, out_specs=out_specs, check_vma=False)
```

profile of v0, /device:TPU:0, one launch (start us, length us, event | category | flops | bytes accessed | tf_op | source)
XLA Modules:
  0.0 140.6 jit_solution(526181429607966376)
XLA Ops:
  6.5 0.0 all-gather.4.cloned.1.call-start
  6.5 1.7 %copy.13 = bf16[1,256,2,256]{3,1,2,0:T(8,128)(2,1)} copy(bf16[1,256,2,256]{3,2,1,0:T(2,128)(2,1)} %param.9) | data formatting | bytes 524288 | tf_op args[3]
  8.2 0.0 all-gather.4.cloned.1.call-update
  8.2 1.1 copy.25
  9.4 7.5 %all_gather.12 = bf16[64,2048]{1,0:T(8,128)(2,1)S(1)} all-gather(bf16[16,2048]{1,0:T(8,128)(2,1)} %param.7), channel_id=1, replica_groups=mesh['section'=2,'blk'=8,'mp'=2] {'section','mp'}, dimensions={0}, use_global_device_ids=true | all-gather | bytes 327680 | tf_op jit(solution)/shard_map/all_gather | solution.py:60
  16.9 0.8 select_reduce_fusion.1
  17.6 0.1 select_reduce_fusion
  17.7 0.2 fusion.18
  17.9 43.4 %all-gather.4.cloned.1.call-done = bf16[1,2048,2,256]{3,1,2,0:T(8,128)(2,1)} async-done(((bf16[1,256,2,256]{3,1,2,0:T(8,128)(2,1)}), bf16[1,2048,2,256]{3,1,2,0:T(8,128)(2,1)}) %all-gather.4.cloned.1.call-update) | async-done | bytes 2097168 | tf_op jit(solution)/shard_map/all_gather | solution.py:78
  61.3 2.1 %fusion.13 = bf16[64,2,256]{2,0,1:T(8,128)(2,1)S(1)} fusion(bf16[1,2048,2,256]{3,1,2,0:T(8,128)(2,1)} %all-gather.4.cloned.1.call-done, bf16[64,2048]{1,0:T(8,128)(2,1)S(1)} %all_gather.12, f32[2048]{0:T(1024)} %param.8, f32[64]{0:T(128)S(1)} %add_rsqrt_fusion), kind=kOutput, calls=%fused_computation.13 | convolution fusion | flops 134774784 | bytes 2433280 | tf_op jit(solution)/shard_map/cr,rtk->ctk/dot_general | solution.py:75
  63.5 30.8 %all-gather.1 = bf16[512,1,256]{2,0,1:T(8,128)(2,1)S(1)} all-gather(bf16[64,1,256]{2,0,1:T(8,128)(2,1)S(1)} %get-tuple-element.5), channel_id=3, replica_groups=mesh['section'=2,'blk'=8,'mp'=2] {'blk'}, dimensions={0}, use_global_device_ids=true | all-gather | bytes 294912 | tf_op jit(solution)/shard_map/all_gather | solution.py:86
  94.3 0.1 reshape.41
  94.4 2.7 %bitcast_reduce_fusion = (f32[128,2,8]{0,2,1:T(8,128)S(1)}, f32[2,512,128,8]{2,1,3,0:T(8,128)}) fusion(pred[512]{0:T(512)(128)(4,1)S(1)} %fusion.28, bf16[128,2,8,128]{3,2,1,0:T(8,128)(2,1)S(1)} %bitcast.42, bf16[512,2,128,1]{2,1,0,3:T(2,128)(2,1)S(1)} %bitcast.43), kind=kOutput, calls=%fused_computation.1 | convolution fusion | flops 271579136 | bytes 4989440 | tf_op jit(solution)/shard_map/qgjd,rgd->qgjr/dot_general | solution.py:37
  97.1 30.8 %all-gather = bf16[512,1,256]{2,0,1:T(8,128)(2,1)S(1)} all-gather(bf16[64,1,256]{2,0,1:T(8,128)(2,1)S(1)} %get-tuple-element.6), channel_id=2, replica_groups=mesh['section'=2,'blk'=8,'mp'=2] {'blk'}, dimensions={0}, use_global_device_ids=true | all-gather | bytes 294912 | tf_op jit(solution)/shard_map/all_gather | solution.py:87
  127.9 0.1 copy.22
  128.0 0.0 copy-start
  128.0 3.4 %fusion.2 = f32[128,2,8]{0,2,1:T(8,128)S(1)} fusion(f32[2,512,128,8]{2,1,3,0:T(8,128)} %get-tuple-element.8, f32[128,2,8]{0,2,1:T(8,128)S(1)} %broadcast_maximum_fusion, pred[512]{0:T(512)(128)(4,1)S(1)} %fusion.28), kind=kLoop, calls=%fused_computation.5 | loop fusion | flops 5240832 | bytes 4211200 | tf_op jit(solution)/shard_map/reduce_sum | solution.py:43
  131.5 0.0 copy-done
  131.5 1.3 divide_convert_fusion
  132.8 1.0 copy.18
  (5 shorter events, 0.0 us)
Async XLA Ops:
  6.5 54.8 %all-gather.4.cloned.1.call-start = ((), (), s32[]{:S(2)}) async-start(), calls=%async_computation | async-start | bytes 2359296 | tf_op jit(solution)/shard_map/all_gather | solution.py:78
  128.0 3.5 %copy-start = (f32[2,512,128,8]{2,1,3,0:T(8,128)S(1)}, f32[2,512,128,8]{2,1,3,0:T(8,128)}, u32[]{:S(2)}) copy-start(f32[2,512,128,8]{2,1,3,0:T(8,128)} %get-tuple-element.8) | copy-start | bytes 12582916
Sparse Core Ops, SparseCore 0:
  9.5 51.7 all-gather.3
where the time goes:
time: 141 us
  blocking collectives  69.1 us (49%)
  waiting for transfers between devices  43.4 us (31%)
  between operations  13.5 us (10%)
  matrix products  6.14 us (4%)
  other arithmetic  4.49 us (3%)
  local copies, waits for them, and re-layouts  4.05 us (3%)
    all_gather x1, waiting for transfers between devices, local(): lax.all_gather(kv_weight, 'blk', axis=1, tiled=True)[0]  43.4 us
    all_gather x1, blocking collectives, local(): lax.all_gather(key_rows, 'blk', axis=0, tiled=True)  30.8 us
    all_gather x1, blocking collectives, local(): lax.all_gather(value_rows, 'blk', axis=0, tiled=True)  30.8 us
    all_gather x1, blocking collectives, local(): lax.all_gather(encoder_states, ('section', 'mp'), axis=0, tiled=True)  7.46 us
    reduce_sum x1, other arithmetic, attend_block(): denominator = jnp.sum(weights, axis=-1)  3.44 us
    unnamed x4, local copies, waits for them, and re-layouts  2.83 us
  transfers between devices with their start and end apart: 1, of which 1 were waited for; matrix products, arithmetic and copies ran while one was open for 2% of the time, Pallas kernels for 0%

commit v1 on v0

--- a/solution.py
+++ b/solution.py
@@ -83,7 +83,9 @@
     final_state = attend(
         start_state,
         query_grid,
-        lax.all_gather(key_rows, "blk", axis=0, tiled=True),
+        jnp.concatenate(
+            lax.all_to_all(jnp.stack([key_rows] * lax.axis_size("blk")), "blk", 0, 0), axis=0
+        ),
         lax.all_gather(value_rows, "blk", axis=0, tiled=True),
         slot_load,
         capacity,

time: 141 us -> 112 us (0.79)
  blocking collectives: 69.1 us -> 39.7 us
  starting transfers between devices: 0.01 us -> 3.41 us
  other arithmetic: 4.49 us -> 2.21 us
  matrix products: 6.14 us -> 4.22 us
    all_gather x1 -> x0, blocking collectives: 30.8 us -> none  [local(): lax.all_gather(key_rows, 'blk', axis=0, tiled=True)]
    all_to_all x0 -> x1, starting transfers between devices: none -> 3.41 us  [local(): lax.all_to_all(jnp.stack([key_rows] * lax.axis_size('blk')), 'blk', 0, 0)]
    reduce_sum x1, other arithmetic: 3.44 us -> 1.16 us  [attend_block(): denominator = jnp.sum(weights, axis=-1)]
    dot_general x1, matrix products: 2.74 us -> 0.81 us  [attend_block(): jnp.einsum('qgjd,rgd->qgjr', query_grid, key_grid, preferred_element_type...]
    all_gather x1, blocking collectives: 30.8 us -> 32.2 us  [local(): lax.all_gather(value_rows, 'blk', axis=0, tiled=True)]
  transfers between devices with their start and end apart: 1 -> 2, of which waited for: 1 -> 1; matrix products, arithmetic and copies ran while one was open for 2% -> 1% of each run, Pallas kernels for 0% -> 0%
where the time goes in v1:
time: 112 us; the launch traced here: 111 us
  waiting for transfers between devices  44.6 us (40%)
  blocking collectives  39.7 us (35%)
  between operations  13.5 us (12%)
  matrix products  4.22 us (4%)
  local copies, waits for them, and re-layouts  3.79 us (3%)
  starting transfers between devices  3.41 us (3%)
  other arithmetic  2.21 us (2%)
    all_gather x1, waiting for transfers between devices, local(): lax.all_gather(kv_weight, 'blk', axis=1, tiled=True)[0]  44.6 us
    all_gather x1, blocking collectives, local(): lax.all_gather(value_rows, 'blk', axis=0, tiled=True)  32.2 us
    all_gather x1, blocking collectives, local(): lax.all_gather(encoder_states, ('section', 'mp'), axis=0, tiled=True)  7.46 us
    all_to_all x1, starting transfers between devices, local(): lax.all_to_all(jnp.stack([key_rows] * lax.axis_size('blk')), 'blk', 0, 0)  3.41 us
  transfers between devices with their start and end apart: 2, of which 1 were waited for; matrix products, arithmetic and copies ran while one was open for 1% of the time, Pallas kernels for 0%

profile of v1, /device:TPU:0, one launch (start us, length us, event | category | flops | bytes accessed | tf_op | source)
XLA Modules:
  0.0 111.4 jit_solution(16267699905086506733)
XLA Ops:
  6.5 0.0 copy-start
  6.5 0.0 all-gather.3.cloned.1.call-start
  6.5 1.7 %copy.18 = bf16[1,256,2,256]{3,1,2,0:T(8,128)(2,1)} copy(bf16[1,256,2,256]{3,2,1,0:T(2,128)(2,1)} %param.9) | data formatting | bytes 524288 | tf_op args[3]
  8.3 0.0 all-gather.3.cloned.1.call-update
  8.3 7.5 %all_gather.9 = bf16[64,2048]{1,0:T(8,128)(2,1)S(1)} all-gather(bf16[16,2048]{1,0:T(8,128)(2,1)} %param.7), channel_id=1, replica_groups=mesh['section'=2,'blk'=8,'mp'=2] {'section','mp'}, dimensions={0}, use_global_device_ids=true | all-gather | bytes 327680 | tf_op jit(solution)/shard_map/all_gather | solution.py:60
  15.8 0.8 select_reduce_fusion.1
  16.6 0.2 fusion.18
  16.7 44.6 %all-gather.3.cloned.1.call-done = bf16[1,2048,2,256]{3,1,2,0:T(8,128)(2,1)} async-done(((bf16[1,256,2,256]{3,1,2,0:T(8,128)(2,1)}), bf16[1,2048,2,256]{3,1,2,0:T(8,128)(2,1)}) %all-gather.3.cloned.1.call-update) | async-done | bytes 2097168 | tf_op jit(solution)/shard_map/all_gather | solution.py:78
  61.3 2.1 %fusion.13 = bf16[64,2,256]{2,0,1:T(8,128)(2,1)S(1)} fusion(bf16[1,2048,2,256]{3,1,2,0:T(8,128)(2,1)} %all-gather.3.cloned.1.call-done, bf16[64,2048]{1,0:T(8,128)(2,1)S(1)} %all_gather.9, f32[2048]{0:T(1024)} %param.8, f32[64]{0:T(128)S(1)} %add_rsqrt_fusion), kind=kOutput, calls=%fused_computation.13 | convolution fusion | flops 134774784 | bytes 2433280 | tf_op jit(solution)/shard_map/cr,rtk->ctk/dot_general | solution.py:75
  63.5 0.7 stack.2
  64.2 3.4 %all-to-all-start = ((bf16[8,64,256]{2,1,0:T(8,128)(2,1)}), bf16[8,64,256]{2,1,0:T(8,128)(2,1)S(1)}, u32[]{:S(2)}, u32[]{:S(2)}) async-start(bf16[8,64,256]{2,1,0:T(8,128)(2,1)} %stack.2), calls=%async_computation | async-start | bytes 524288 | tf_op jit(solution)/shard_map/all_to_all | solution.py:87
  67.6 0.0 copy-done
  67.6 0.1 copy.30
  67.8 0.1 select_reduce_fusion
  67.9 32.2 %all-gather = bf16[512,1,256]{2,0,1:T(8,128)(2,1)S(1)} all-gather(bf16[64,1,256]{2,0,1:T(8,128)(2,1)S(1)} %get-tuple-element.6), channel_id=2, replica_groups=mesh['section'=2,'blk'=8,'mp'=2] {'blk'}, dimensions={0}, use_global_device_ids=true | all-gather | bytes 294912 | tf_op jit(solution)/shard_map/all_gather | solution.py:89
  100.1 0.1 copy.27
  100.2 0.0 all-to-all-done
  100.2 0.1 reshape_reshape.3
  100.3 0.8 bitcast_reduce_fusion
  101.1 1.2 %fusion.2 = f32[128,2,8]{0,2,1:T(8,128)S(1)} fusion(f32[2,512,128,8]{2,1,3,0:T(8,128)S(1)} %get-tuple-element.8, f32[128,2,8]{0,2,1:T(8,128)S(1)} %broadcast_maximum_fusion, pred[512]{0:T(512)(128)(4,1)S(1)} %fusion.28), kind=kLoop, calls=%fused_computation.5 | loop fusion | flops 5240832 | bytes 4211200 | tf_op jit(solution)/shard_map/reduce_sum | solution.py:43
  102.3 1.3 %divide_convert_fusion = bf16[128,2,8,128]{0,3,2,1:T(8,128)(2,1)S(1)} fusion(bf16[512,2,128,1]{0,2,3,1:T(8,128)(2,1)S(1)} %bitcast.46, f32[2,512,128,8]{2,1,3,0:T(8,128)S(1)} %get-tuple-element.8, f32[128,2,8]{0,2,1:T(8,128)S(1)} %broadcast_maximum_fusion, pred[512]{0:T(512)(128)(4,1)S(1)} %fusion.28, f32[128,2,8]{0,2,1:T(8,128)S(1)} %fusion.2), kind=kOutput, calls=%fused_computation.14 | convolution fusion | flops 274202624 | bytes 4997632 | tf_op jit(solution)/shard_map/qgjr,rgd->qgjd/dot_general | solution.py:44
  103.6 1.0 copy.23
  (5 shorter events, 0.0 us)
Async XLA Ops:
  6.5 61.1 %copy-start = (bf16[1,128,2048]{2,1,0:T(8,128)(2,1)S(1)}, bf16[1,128,2048]{2,1,0:T(8,128)(2,1)}, u32[]{:S(2)}) copy-start(bf16[1,128,2048]{2,1,0:T(8,128)(2,1)} %param.6) | copy-start | bytes 1572868
  6.5 54.8 %all-gather.3.cloned.1.call-start = ((), (), s32[]{:S(2)}) async-start(), calls=%async_computation.1 | async-start | bytes 2359296 | tf_op jit(solution)/shard_map/all_gather | solution.py:78
  64.2 36.0 %all-to-all-start = ((bf16[8,64,256]{2,1,0:T(8,128)(2,1)}), bf16[8,64,256]{2,1,0:T(8,128)(2,1)S(1)}, u32[]{:S(2)}, u32[]{:S(2)}) async-start(bf16[8,64,256]{2,1,0:T(8,128)(2,1)} %stack.2), calls=%async_computation | async-start | bytes 524288 | tf_op jit(solution)/shard_map/all_to_all | solution.py:87
Sparse Core Ops, SparseCore 0:
  9.5 51.7 all-gather.2
